TPU v7x, 512 devices: a whole 4x8x8 slice. The times are simulated.
512 devices in a mesh: elem: 32 (over z, y_lo), mode: 16 (over x, y_hi, core).
Axes of the slice: x: 4, y: 8 (y_hi: 2, y_lo: 4; y = y_hi * 4 + y_lo), z: 8, core: 2. Of those that a mesh axis runs over, the one named last changes fastest.
Arguments:
- modal_history: float32 [4096, 512], P('elem', 'mode'), may hold values from -6 to 6
- stress_modes: float32 [512, 6144], P('mode', 'elem'), may hold values from -0.5 to 0.5
Outputs:
- stress_spectrum: float32 [6144, 2, 2048], P(('elem', 'mode'))
All inputs are finite; a program needn't handle non-finite values.
Results may differ from a plain program's by a relative error of at most 0.00007.
Values sent between devices are 32-bit elements; how exact they have to be, the bound alone decides.
No kernel may reach another device: no remote copies, remote signals or barrier semaphores. Data moves between devices by JAX's collectives and lax.ppermute only.
A program may use at most 64 MiB of HBM per device.

v0:
```python
import math
import jax
import jax.numpy as jnp
from jax import lax
from jax.sharding import PartitionSpec as P

highest = lax.Precision.HIGHEST


def spectra(signal):
    columns = signal.shape[0]
    radix = 64
    halved = radix // 2
    blocked = signal.reshape(columns, radix, radix)
    counter = jnp.arange(radix, dtype=jnp.int32)
    products = counter[:, None] * counter[None, :]
    small_angle = (products % radix).astype(jnp.float32) * (2.0 * math.pi / radix)
    cosine_small = jnp.cos(small_angle)
    sine_small = jnp.sin(small_angle)
    twist_angle = (products % (radix * radix)).astype(jnp.float32) * (
        2.0 * math.pi / (radix * radix)
    )
    twist_cos = jnp.cos(twist_angle)
    twist_sin = jnp.sin(twist_angle)
    first_real = jnp.einsum("cab,ak->cbk", blocked, cosine_small, precision=highest)
    first_imag = -jnp.einsum("cab,ak->cbk", blocked, sine_small, precision=highest)
    turned_real = first_real * twist_cos + first_imag * twist_sin
    turned_imag = first_imag * twist_cos - first_real * twist_sin
    cosine_half = cosine_small[:, :halved]
    sine_half = sine_small[:, :halved]
    final_real = jnp.einsum(
        "cbk,bj->cjk", turned_real, cosine_half, precision=highest
    ) + jnp.einsum("cbk,bj->cjk", turned_imag, sine_half, precision=highest)
    final_imag = jnp.einsum(
        "cbk,bj->cjk", turned_imag, cosine_half, precision=highest
    ) - jnp.einsum("cbk,bj->cjk", turned_real, sine_half, precision=highest)
    stacked = jnp.stack([final_real, final_imag], axis=1) * (1.0 / radix)
    return stacked.reshape(columns, 2, halved * radix)


def per_device(modal_history, stress_modes):
    elem_count = lax.axis_size("elem")
    mode_count = lax.axis_size("mode")
    local_steps = modal_history.shape[0]
    partial_value = jnp.einsum(
        "mp,tm->pt",
        lax.all_gather(stress_modes, "elem", axis=1, tiled=True),
        modal_history,
        precision=highest,
        preferred_element_type=jnp.float32,
    )
    owned_width = partial_value.shape[0] // (elem_count * mode_count)
    reordered = partial_value.reshape(elem_count, mode_count, owned_width, local_steps)
    reordered = reordered.transpose(1, 0, 2, 3).reshape(
        mode_count * elem_count * owned_width, local_steps
    )
    summed = lax.psum_scatter(reordered, "mode", scatter_dimension=0, tiled=True)
    stress = lax.all_to_all(summed, "elem", split_axis=0, concat_axis=1, tiled=True)
    return spectra(stress)


def solution(mesh):
    placed = (P("elem", "mode"), P("mode", "elem"))
    return jax.shard_map(
        per_device,
        mesh=mesh,
        in_specs=placed,
        out_specs=P(("elem", "mode"), None, None),
        check_vma=False,
    )
```

profile of v0, /device:TPU:2, one launch (start us, length us, event | category | flops | bytes accessed | tf_op | source)
XLA Modules:
  0.0 250.8 jit_solution(8755520814195808711)
XLA Ops:
  6.5 0.0 copy-start
  6.5 0.0 reduce-scatter.2.cloned.1.call-start
  6.5 95.5 %all-gather = f32[32,192,32]{1,2,0:T(8,128)S(1)} all-gather(f32[1,192,32]{1,2,0:T(8,128)} %bitcast.31), channel_id=1, replica_groups=mesh['elem'=32,'mode'=16] {'elem'}, dimensions={0}, use_global_device_ids=true | all-gather | bytes 811008 | tf_op jit(solution)/shard_map/all_gather | solution.py:47
  102.0 0.6 copy.19
  102.6 1.3 reshape.58
  103.9 0.0 copy-done
  103.9 6.2 %fusion.32 = f32[6144,128]{1,0:T(8,128)S(1)} fusion(f32[6144,32]{0,1:T(8,128)} %reshape.58, f32[128,32]{0,1:T(8,128)S(1)} %copy-done), kind=kOutput, calls=%fused_computation.44 | convolution fusion | flops 301989888 | bytes 3948544 | tf_op jit(solution)/shard_map/mp,tm->pt/dot_general | solution.py:45
  110.1 2.1 reshape.54
  112.2 4.6 %copy.20 = f32[16,32,12,128]{3,2,1,0:T(8,128)} copy(f32[16,32,12,128]{3,2,0,1:T(8,128)} %bitcast.29) | data formatting | bytes 6291456 | tf_op jit(solution)/shard_map/transpose | solution.py:54
  116.8 4.6 %reshape.55 = f32[6144,128]{1,0:T(8,128)} reshape(f32[16,32,12,128]{3,2,1,0:T(8,128)} %copy.20) | data formatting | bytes 6291456 | tf_op jit(solution)/shard_map/reshape | solution.py:54
  121.4 0.0 reduce-scatter.2.cloned.1.call-update
  121.4 94.8 %reduce-scatter.2.cloned.1.call-done = f32[384,128]{1,0:T(8,128)} async-done(((f32[6144,128]{1,0:T(8,128)}), f32[384,128]{1,0:T(8,128)}) %reduce-scatter.2.cloned.1.call-update) | async-done | bytes 196624 | tf_op jit(solution)/shard_map/reduce_scatter | solution.py:57
  216.2 1.6 all_to_all.12
  217.9 9.7 %all-to-all-start = ((f32[32,12,128]{2,1,0:T(8,128)}), f32[32,12,128]{2,1,0:T(8,128)S(1)}, u32[]{:S(2)}, u32[]{:S(2)}) async-start(f32[32,12,128]{2,1,0:T(8,128)} %all_to_all.12), calls=%async_computation.1 | async-start | bytes 524288 | tf_op jit(solution)/shard_map/all_to_all | solution.py:58
  227.6 0.1 fusion.19
  227.7 0.1 copy.24
  227.8 0.1 fusion.18
  228.0 0.1 copy.27
  228.1 0.2 fusion.21
  228.2 0.1 fusion.20
  228.4 11.2 %all-to-all-done = f32[32,12,128]{2,1,0:T(8,128)S(1)} async-done(((f32[32,12,128]{2,1,0:T(8,128)}), f32[32,12,128]{2,1,0:T(8,128)S(1)}, u32[]{:S(2)}, u32[]{:S(2)}) %all-to-all-start) | async-done | bytes 196640 | tf_op jit(solution)/shard_map/all_to_all | solution.py:58
  239.5 0.1 copy.21
  239.6 0.1 reshape.56
  239.7 0.8 convolution_negate_fusion
  240.6 0.8 fusion.9
  241.4 0.4 fusion.2
  241.7 0.4 fusion.3
  242.1 0.4 fusion.1
  242.5 0.1 stack.9
  242.6 0.4 fusion
  242.9 0.1 stack.10
  243.1 0.8 copy.28
  (1 shorter events, 0.0 us)
Async XLA Ops:
  6.5 97.4 %copy-start = (f32[128,32]{0,1:T(8,128)S(1)}, f32[128,32]{0,1:T(8,128)}, u32[]{:S(2)}) copy-start(f32[128,32]{0,1:T(8,128)} %param.2) | copy-start | bytes 49156
  6.5 209.7 %reduce-scatter.2.cloned.1.call-start = ((), (), s32[]{:S(2)}) async-start(), calls=%async_computation.2 | async-start | bytes 3342336 | tf_op jit(solution)/shard_map/reduce_scatter | solution.py:57
  217.9 21.7 %all-to-all-start = ((f32[32,12,128]{2,1,0:T(8,128)}), f32[32,12,128]{2,1,0:T(8,128)S(1)}, u32[]{:S(2)}, u32[]{:S(2)}) async-start(f32[32,12,128]{2,1,0:T(8,128)} %all_to_all.12), calls=%async_computation.1 | async-start | bytes 524288 | tf_op jit(solution)/shard_map/all_to_all | solution.py:58
Sparse Core Ops, SparseCore 0:
  121.6 94.6 reduce-scatter.1
where the time goes:
time: 251 us
  waiting for transfers between devices  106 us (42%)
  blocking collectives  95.5 us (38%)
  local copies, waits for them, and re-layouts  16.2 us (6%)
  between operations  13.5 us (5%)
  starting transfers between devices  9.72 us (4%)
  matrix products  9.24 us (4%)
    all_gather x1, blocking collectives, per_device(): lax.all_gather(stress_modes, 'elem', axis=1, tiled=True)  95.5 us
    reduce_scatter x1, waiting for transfers between devices, per_device(): lax.psum_scatter(reordered, 'mode', scatter_dimension=0, tiled=True)  94.8 us
    all_to_all x1, waiting for transfers between devices, per_device(): lax.all_to_all(summed, 'elem', split_axis=0, concat_axis=1, tiled=True)  11.2 us
    all_to_all x1, starting transfers between devices, per_device(): lax.all_to_all(summed, 'elem', split_axis=0, concat_axis=1, tiled=True)  9.72 us
    dot_general x1, matrix products, per_device(): jnp.einsum('mp,tm->pt', lax.all_gather(stress_modes, 'elem', axis=1, tile...  6.19 us
  transfers between devices with their start and end apart: 2, of which 2 were waited for; matrix products, arithmetic and copies ran while one was open for 0% of the time, Pallas kernels for 0%

commit v1 on v0

--- a/solution.py
+++ b/solution.py
@@ -44,7 +44,9 @@
     local_steps = modal_history.shape[0]
     partial_value = jnp.einsum(
         "mp,tm->pt",
-        lax.all_gather(stress_modes, "elem", axis=1, tiled=True),
+        jnp.concatenate(
+            lax.all_to_all(jnp.stack([stress_modes] * lax.axis_size("elem")), "elem", 0, 0), axis=1
+        ),
         modal_history,
         precision=highest,
         preferred_element_type=jnp.float32,

time: 251 us -> 210 us (0.84)
  blocking collectives: 95.5 us -> 40.9 us
  local copies, waits for them, and re-layouts: 16.2 us -> 29.9 us
  matrix products: 9.24 us -> 5.8 us
  waiting for transfers between devices: 106 us -> 109 us
    all_gather x1 -> x0, blocking collectives: 95.5 us -> none  [per_device(): lax.all_gather(stress_modes, 'elem', axis=1, tiled=True)]
    all_to_all x0 -> x1, blocking collectives: none -> 40.9 us  [per_device(): lax.all_to_all(jnp.stack([stress_modes] * lax.axis_size('elem')), 'elem',...]
    dot_general x0 -> x2, local copies, waits for them, and re-layouts: none -> 17.4 us  [per_device(): jnp.einsum('mp,tm->pt', jnp.concatenate(lax.all_to_all(jnp.stack([stress_...]
    dot_general x1, matrix products: 6.19 us -> 2.75 us  [per_device(): jnp.einsum('mp,tm->pt', jnp.concatenate(lax.all_to_all(jnp.stack([stress_...]
    reduce_scatter x1, waiting for transfers between devices: 94.8 us -> 97.7 us  [per_device(): lax.psum_scatter(reordered, 'mode', scatter_dimension=0, tiled=True)]
where the time goes in v1:
time: 210 us; the launch traced here: 209 us
  waiting for transfers between devices  109 us (52%)
  blocking collectives  40.9 us (19%)
  local copies, waits for them, and re-layouts  29.9 us (14%)
  between operations  13.5 us (6%)
  starting transfers between devices  9.89 us (5%)
  matrix products  5.8 us (3%)
    reduce_scatter x1, waiting for transfers between devices, per_device(): lax.psum_scatter(reordered, 'mode', scatter_dimension=0, tiled=True)  97.7 us
    all_to_all x1, blocking collectives, per_device(): lax.all_to_all(jnp.stack([stress_modes] * lax.axis_size('elem')), 'elem',...  40.9 us
    dot_general x2, local copies, waits for them, and re-layouts, per_device(): jnp.einsum('mp,tm->pt', jnp.concatenate(lax.all_to_all(jnp.stack([stress_...  17.4 us
    all_to_all x1, waiting for transfers between devices, per_device(): lax.all_to_all(summed, 'elem', split_axis=0, concat_axis=1, tiled=True)  11 us
    all_to_all x1, starting transfers between devices, per_device(): lax.all_to_all(summed, 'elem', split_axis=0, concat_axis=1, tiled=True)  9.89 us
    reshape x1, local copies, waits for them, and re-layouts, per_device(): reordered.transpose(1, 0, 2, 3)  4.59 us
  transfers between devices with their start and end apart: 2, of which 2 were waited for; matrix products, arithmetic and copies ran while one was open for 0% of the time, Pallas kernels for 0%

profile of v1, /device:TPU:2, one launch (start us, length us, event | category | flops | bytes accessed | tf_op | source)
XLA Modules:
  0.0 209.4 jit_solution(10778998492722708715)
XLA Ops:
  6.5 0.0 copy-start
  6.5 0.0 reduce-scatter.2.cloned.1.call-start
  6.5 0.9 stack.8
  7.4 40.9 %all_to_all.21 = f32[32,32,192]{2,1,0:T(8,128)S(1)} all-to-all(f32[32,32,192]{2,1,0:T(8,128)S(1)} %stack.8), channel_id=1, replica_groups=mesh['elem'=32,'mode'=16] {'elem'}, dimensions={0} | all-to-all | bytes 1572864 | tf_op jit(solution)/shard_map/all_to_all | solution.py:48
  48.4 0.6 copy.20
  49.0 0.4 reshape.62
  49.4 10.6 %reshape.70 = f32[32,16,12,32]{2,1,0,3:T(8,128)} reshape(f32[6144,32]{0,1:T(8,128)S(1)} %bitcast.34) | data formatting | bytes 1572864 | tf_op jit(solution)/shard_map/mp,tm->pt/dot_general | solution.py:45
  60.0 6.9 %copy.22 = f32[32,16,12,32]{3,1,2,0:T(8,128)S(1)} copy(f32[32,16,12,32]{2,1,0,3:T(8,128)} %reshape.70) | data formatting | bytes 1572864 | tf_op jit(solution)/shard_map/mp,tm->pt/dot_general | solution.py:45
  66.8 0.0 copy-done
  66.8 2.7 %convolution_bitcast_fusion = f32[16,32,12,128]{3,0,2,1:T(8,128)S(1)} fusion(f32[32,16,12,32]{3,1,2,0:T(8,128)S(1)} %copy.22, f32[128,32]{0,1:T(8,128)S(1)} %copy-done), kind=kOutput, calls=%fused_computation | convolution fusion | flops 301989888 | bytes 3948544 | tf_op jit(solution)/shard_map/mp,tm->pt/dot_general | solution.py:45
  69.6 3.0 %copy.23 = f32[16,32,12,128]{3,2,1,0:T(8,128)} copy(f32[16,32,12,128]{3,0,2,1:T(8,128)S(1)} %convolution_bitcast_fusion) | data formatting | bytes 6291456 | tf_op jit(solution)/shard_map/transpose | solution.py:56
  72.6 4.6 %reshape.63 = f32[6144,128]{1,0:T(8,128)} reshape(f32[16,32,12,128]{3,2,1,0:T(8,128)} %copy.23) | data formatting | bytes 6291456 | tf_op jit(solution)/shard_map/reshape | solution.py:56
  77.2 0.0 reduce-scatter.2.cloned.1.call-update
  77.2 97.7 %reduce-scatter.2.cloned.1.call-done = f32[384,128]{1,0:T(8,128)} async-done(((f32[6144,128]{1,0:T(8,128)}), f32[384,128]{1,0:T(8,128)}) %reduce-scatter.2.cloned.1.call-update) | async-done | bytes 196624 | tf_op jit(solution)/shard_map/reduce_scatter | solution.py:59
  174.9 1.6 all_to_all.16
  176.5 9.9 %all-to-all-start.1 = ((f32[32,12,128]{2,1,0:T(8,128)}), f32[32,12,128]{2,1,0:T(8,128)S(1)}, u32[]{:S(2)}, u32[]{:S(2)}) async-start(f32[32,12,128]{2,1,0:T(8,128)} %all_to_all.16), calls=%async_computation.2 | async-start | bytes 524288 | tf_op jit(solution)/shard_map/all_to_all | solution.py:60
  186.4 0.1 fusion.20
  186.6 0.1 copy.27
  186.6 0.1 fusion.19
  186.8 0.1 copy.30
  186.9 0.2 fusion.22
  187.0 0.1 fusion.21
  187.2 11.0 %all-to-all-done.1 = f32[32,12,128]{2,1,0:T(8,128)S(1)} async-done(((f32[32,12,128]{2,1,0:T(8,128)}), f32[32,12,128]{2,1,0:T(8,128)S(1)}, u32[]{:S(2)}, u32[]{:S(2)}) %all-to-all-start.1) | async-done | bytes 196640 | tf_op jit(solution)/shard_map/all_to_all | solution.py:60
  198.2 0.1 copy.24
  198.2 0.1 reshape.64
  198.4 0.8 convolution_negate_fusion
  199.2 0.8 fusion.9
  200.0 0.4 fusion.2
  200.4 0.4 fusion.3
  200.7 0.4 fusion.1
  201.1 0.1 stack.9
  201.2 0.4 fusion
  201.6 0.1 stack.10
  201.7 0.8 copy.31
  (1 shorter events, 0.0 us)
Async XLA Ops:
  6.5 60.3 %copy-start = (f32[128,32]{0,1:T(8,128)S(1)}, f32[128,32]{0,1:T(8,128)}, u32[]{:S(2)}) copy-start(f32[128,32]{0,1:T(8,128)} %param.2) | copy-start | bytes 49156
  6.5 168.3 %reduce-scatter.2.cloned.1.call-start = ((), (), s32[]{:S(2)}) async-start(), calls=%async_computation.3 | async-start | bytes 3342336 | tf_op jit(solution)/shard_map/reduce_scatter | solution.py:59
  176.5 21.7 %all-to-all-start.1 = ((f32[32,12,128]{2,1,0:T(8,128)}), f32[32,12,128]{2,1,0:T(8,128)S(1)}, u32[]{:S(2)}, u32[]{:S(2)}) async-start(f32[32,12,128]{2,1,0:T(8,128)} %all_to_all.16), calls=%async_computation.2 | async-start | bytes 524288 | tf_op jit(solution)/shard_map/all_to_all | solution.py:60
Sparse Core Ops, SparseCore 0:
  77.3 97.5 reduce-scatter.1
